TPU v7x, 512 devices: a whole 4x4x16 slice. The times are simulated.
512 devices in a mesh: kpt: 16 (over x, y_lo, core), aux: 32 (over z, y_hi).
Axes of the slice: x: 4, y: 4 (y_hi: 2, y_lo: 2; y = y_hi * 2 + y_lo), z: 16, core: 2. Of those that a mesh axis runs over, the one named last changes fastest.
Arguments:
- orbitals: bfloat16 [16, 768, 384], P('kpt', 'aux'), may hold values from -6 to 6
- fitted: bfloat16 [16, 2, 64, 768, 768], P('kpt', None, 'aux'), may hold values from -0.21875 to 0.21875
- kpoint_pair_index: int32 [16, 4], P('kpt'), may hold values from 0 to 1
Outputs:
- exchange_images: float32 [2, 16, 768, 384], P(None, 'kpt', 'aux')
- orbitals_out: float32 [16, 768, 384], P('kpt', 'aux')
Inputs may be any that keep to these rules, and one draw needn't show every extreme that they name: kpoint_pair_index[k, v] names which of the 2 fitted tensors of k-point k serves visit v.
All inputs are finite; a program needn't handle non-finite values.
Results may differ from a plain program's by a relative error of at most 0.0011.
Values may be sent and summed in bfloat16 or wider, within the bound.
A program may use at most 64 MiB of HBM per device.

v0:
```python
import jax
import jax.numpy as jnp
from jax import lax
from jax.sharding import PartitionSpec as P

VISIT_COUNT = 4
update_fraction = 0.25


def passed_along(value, axis, by):
    count = lax.axis_size(axis)
    return lax.ppermute(value, axis, [(i, (i + by) % count) for i in range(count)])


def half_transform(slot_block, paired_kpoint):
    layers = slot_block.shape[0]
    flattened = slot_block.reshape(layers * slot_block.shape[1], slot_block.shape[2])
    half_done = jnp.dot(flattened, paired_kpoint, preferred_element_type=jnp.float32).astype(
        jnp.bfloat16
    )
    return half_done.reshape(layers, slot_block.shape[1], paired_kpoint.shape[1])


def on_device(orbitals, fitted, kpoint_pair_index):
    rows_here = orbitals.shape[1]
    norm_scale = 1.0 / (fitted.shape[2] * lax.axis_size("aux") * orbitals.shape[2])
    current = orbitals[0].astype(jnp.float32)
    fitted_point = fitted[0]
    applied_list = []
    for outer in range(VISIT_COUNT // 2):
        offset = outer + 1
        rounded = current.astype(jnp.bfloat16)
        own_full = lax.all_gather(rounded, "aux", axis=0, tiled=True)
        trailing = passed_along(own_full, "kpt", offset)
        leading = passed_along(own_full, "kpt", -offset)
        slot_first = lax.dynamic_index_in_dim(
            fitted_point, kpoint_pair_index[0, 2 * outer], 0, keepdims=False
        )
        slot_second = lax.dynamic_index_in_dim(
            fitted_point, kpoint_pair_index[0, 2 * outer + 1], 0, keepdims=False
        )
        half_done = jnp.concatenate(
            (half_transform(slot_first, trailing), half_transform(slot_second, leading)), axis=0
        )
        inner_block = jnp.einsum(
            "pmi,mj->pij", half_done, own_full, preferred_element_type=jnp.float32
        ).astype(jnp.bfloat16)
        partial_sum = jnp.einsum(
            "pmi,pij->mj", half_done, inner_block, preferred_element_type=jnp.float32
        )
        summed = lax.psum(partial_sum, "aux")
        applied = lax.dynamic_slice_in_dim(summed, lax.axis_index("aux") * rows_here, rows_here, 0)
        applied = applied * norm_scale
        applied_list.append(applied)
        current = current - update_fraction * applied
    return (jnp.stack(applied_list)[:, None], current[None])


def solution(mesh):
    placed = (P("kpt", "aux", None), P("kpt", None, "aux", None, None), P("kpt", None))
    return jax.shard_map(
        on_device,
        mesh=mesh,
        in_specs=placed,
        out_specs=(P(None, "kpt", "aux", None), P("kpt", "aux", None)),
        check_vma=False,
    )
```

profile of v0, /device:TPU:6, one launch (start us, length us, event | category | flops | bytes accessed | tf_op | source)
XLA Modules:
  0.0 860.2 jit_solution(11143747537137993466)
XLA Ops:
  7.2 0.0 all-reduce.3.cloned.1.call-start
  7.2 86.2 %all-gather = bf16[1,768,384]{2,1,0:T(8,128)(2,1)S(1)} all-gather(bf16[1,24,384]{2,1,0:T(8,128)(2,1)} %param.3), channel_id=2, replica_groups=mesh['kpt'=16,'aux'=32] {'aux'}, dimensions={1}, use_global_device_ids=true | all-gather | bytes 608256 | tf_op jit(solution)/shard_map/all_gather | solution.py:33
  93.4 1.9 collective-permute-start
  95.3 4.5 collective-permute-start.1
  99.9 1.5 fusion.13
  109.1 5.9 constant_dynamic-slice_fusion.1
  115.0 0.0 collective-permute-done
  115.0 3.5 convolution_convert_fusion.3
  118.5 0.0 collective-permute-done.1
  118.5 3.5 convolution_convert_fusion.2
  122.0 0.0 copy-start
  122.0 6.1 fusion.2
  128.0 0.0 all-reduce.3.cloned.1.call-update
  128.0 0.0 all-reduce.5.cloned.1.call-start
  128.1 304.9 %all-reduce.3.cloned.1.call-done = f32[768,384]{1,0:T(8,128)} async-done(((f32[768,384]{1,0:T(8,128)}), f32[768,384]{1,0:T(8,128)}) %all-reduce.3.cloned.1.call-update) | async-done | bytes 1179664 | tf_op jit(solution)/shard_map/psum | solution.py:51
  433.0 0.0 copy-done
  433.0 0.8 fusion.8
  433.8 79.0 %all_gather.7 = bf16[768,384]{1,0:T(8,128)(2,1)S(1)} all-gather(bf16[24,384]{1,0:T(8,128)(2,1)S(1)} %fusion.8), channel_id=1, replica_groups=mesh['kpt'=16,'aux'=32] {'aux'}, dimensions={0}, use_global_device_ids=true | all-gather | bytes 608256 | tf_op jit(solution)/shard_map/all_gather | solution.py:33
  512.8 3.0 collective-permute-start.2
  515.7 3.7 collective-permute-start.3
  519.5 9.9 %collective-permute-done.2 = bf16[768,384]{1,0:T(8,128)(2,1)S(1)} collective-permute-done((bf16[768,384]{1,0:T(8,128)(2,1)S(1)}, bf16[768,384]{1,0:T(8,128)(2,1)S(1)}, u32[]{:S(2)}, u32[]{:S(2)}) %collective-permute-start.2) | collective-permute-done | bytes 589856 | tf_op jit(solution)/shard_map/ppermute | solution.py:12
  529.4 4.1 convolution_convert_fusion.1
  533.6 0.0 collective-permute-done.3
  533.6 2.5 convolution_convert_fusion
  536.0 6.0 fusion.3
  542.1 0.0 all-reduce.5.cloned.1.call-update
  542.1 309.2 %all-reduce.5.cloned.1.call-done = f32[768,384]{1,0:T(8,128)} async-done(((f32[768,384]{1,0:T(8,128)}), f32[768,384]{1,0:T(8,128)}) %all-reduce.5.cloned.1.call-update) | async-done | bytes 1179664 | tf_op jit(solution)/shard_map/psum | solution.py:51
  851.3 1.4 subtract_bitcast_fusion
  852.7 0.6 maximum_bitcast_fusion
Async XLA Ops:
  7.2 425.8 %all-reduce.3.cloned.1.call-start = ((), (), s32[]{:S(2)}) async-start(), calls=%async_computation | async-start | bytes 2359296 | tf_op jit(solution)/shard_map/psum | solution.py:51
  93.4 21.6 %collective-permute-start = (bf16[768,384]{1,0:T(8,128)(2,1)S(1)}, bf16[768,384]{1,0:T(8,128)(2,1)}, u32[]{:S(2)}, u32[]{:S(2)}) collective-permute-start(bf16[768,384]{1,0:T(8,128)(2,1)S(1)} %bitcast.51), channel_id=1, source_target_pairs={{0,32},{32,64},{64,96},{96,128},{128,160},{160,192},{192,224},{224... | collective-permute-start | bytes 1769480 | tf_op jit(solution)/shard_map/ppermute | solution.py:12
  95.3 23.1 %collective-permute-start.1 = (bf16[768,384]{1,0:T(8,128)(2,1)S(1)}, bf16[768,384]{1,0:T(8,128)(2,1)}, u32[]{:S(2)}, u32[]{:S(2)}) collective-permute-start(bf16[768,384]{1,0:T(8,128)(2,1)S(1)} %bitcast.52), channel_id=1, source_target_pairs={{0,480},{32,0},{64,32},{96,64},{128,96},{160,128},{192,160},{224,1... | collective-permute-start | bytes 1769480 | tf_op jit(solution)/shard_map/ppermute | solution.py:12
  122.0 311.0 %copy-start = (bf16[1,24,384]{2,1,0:T(8,128)(2,1)S(1)}, bf16[1,24,384]{2,1,0:T(8,128)(2,1)}, u32[]{:S(2)}) copy-start(bf16[1,24,384]{2,1,0:T(8,128)(2,1)} %param.3) | copy-start | bytes 55300
  128.0 723.3 %all-reduce.5.cloned.1.call-start = ((), (), s32[]{:S(2)}) async-start(), calls=%async_computation.1 | async-start | bytes 2359296 | tf_op jit(solution)/shard_map/psum | solution.py:51
  512.8 16.7 %collective-permute-start.2 = (bf16[768,384]{1,0:T(8,128)(2,1)S(1)}, bf16[768,384]{1,0:T(8,128)(2,1)S(1)}, u32[]{:S(2)}, u32[]{:S(2)}) collective-permute-start(bf16[768,384]{1,0:T(8,128)(2,1)S(1)} %all_gather.7), channel_id=1, source_target_pairs={{0,64},{32,96},{64,128},{96,160},{128,192},{160,224},{192,256},{22... | collective-permute-start | bytes 1769480 | tf_op jit(solution)/shard_map/ppermute | solution.py:12
  515.7 17.8 %collective-permute-start.3 = (bf16[768,384]{1,0:T(8,128)(2,1)S(1)}, bf16[768,384]{1,0:T(8,128)(2,1)S(1)}, u32[]{:S(2)}, u32[]{:S(2)}) collective-permute-start(bf16[768,384]{1,0:T(8,128)(2,1)S(1)} %all_gather.7), channel_id=1, source_target_pairs={{0,448},{32,480},{64,0},{96,32},{128,64},{160,96},{192,128},{224,1... | collective-permute-start | bytes 1769480 | tf_op jit(solution)/shard_map/ppermute | solution.py:12
Sparse Core Ops, SparseCore 0:
  128.2 304.7 all-reduce.2
  542.2 309.0 all-reduce.4
where the time goes:
time: 861 us; the launch traced here: 860 us
  waiting for transfers between devices  624 us (72%)
  blocking collectives  165 us (19%)
  matrix products  25.6 us (3%)
  between operations  21.8 us (3%)
  starting transfers between devices  13.3 us (2%)
    psum x2, waiting for transfers between devices, on_device(): summed = lax.psum(partial_sum, 'aux')  614 us
    all_gather x2, blocking collectives, on_device(): own_full = lax.all_gather(rounded, 'aux', axis=0, tiled=True)  165 us
  transfers between devices with their start and end apart: 6, of which 3 were waited for; matrix products, arithmetic and copies ran while one was open for 2% of the time, Pallas kernels for 0%

commit v1 on v0

--- a/solution.py
+++ b/solution.py
@@ -2,9 +2,16 @@
 import jax.numpy as jnp
 from jax import lax
 from jax.sharding import PartitionSpec as P
+from jax.lax import all_to_all, axis_size
 
 VISIT_COUNT = 4
 update_fraction = 0.25
+
+
+def finish_frame(frame):
+    v_next = jnp.stack([frame for _ in range(axis_size("aux"))], axis=0)
+    local_out = all_to_all(v_next, "aux", 0, 0)
+    return jnp.concatenate(local_out, axis=0)
 
 
 def passed_along(value, axis, by):
@@ -30,7 +37,7 @@
     for outer in range(VISIT_COUNT // 2):
         offset = outer + 1
         rounded = current.astype(jnp.bfloat16)
-        own_full = lax.all_gather(rounded, "aux", axis=0, tiled=True)
+        own_full = finish_frame(rounded)
         trailing = passed_along(own_full, "kpt", offset)
         leading = passed_along(own_full, "kpt", -offset)
         slot_first = lax.dynamic_index_in_dim(

time: 861 us -> 777 us (0.902)
  blocking collectives: 165 us -> 88 us
    all_gather x2 -> x0, blocking collectives: 165 us -> none  [on_device(): own_full = lax.all_gather(rounded, 'aux', axis=0, tiled=True)]
    all_to_all x0 -> x2, blocking collectives: none -> 88 us  [finish_frame(): local_out = all_to_all(v_next, 'aux', 0, 0)]
where the time goes in v1:
time: 777 us; the launch traced here: 776 us
  waiting for transfers between devices  617 us (79%)
  blocking collectives  88 us (11%)
  matrix products  24.6 us (3%)
  between operations  21.9 us (3%)
  starting transfers between devices  13.3 us (2%)
  local copies, waits for them, and re-layouts  8.19 us (1%)
    psum x2, waiting for transfers between devices, on_device(): summed = lax.psum(partial_sum, 'aux')  608 us
    all_to_all x2, blocking collectives, finish_frame(): local_out = all_to_all(v_next, 'aux', 0, 0)  88 us
  transfers between devices with their start and end apart: 6, of which 3 were waited for; matrix products, arithmetic and copies ran while one was open for 2% of the time, Pallas kernels for 0%

profile of v1, /device:TPU:6, one launch (start us, length us, event | category | flops | bytes accessed | tf_op | source)
XLA Modules:
  0.0 776.2 jit_solution(11099411661791189887)
XLA Ops:
  7.2 0.0 all-reduce.3.cloned.1.call-start
  7.2 0.8 stack.13
  8.0 53.7 %all_to_all.10 = bf16[32,24,384]{2,1,0:T(8,128)(2,1)S(1)} all-to-all(bf16[32,24,384]{2,1,0:T(8,128)(2,1)S(1)} %stack.13), channel_id=1, replica_groups=mesh['kpt'=16,'aux'=32] {'aux'}, dimensions={0} | all-to-all | bytes 1179648 | tf_op jit(solution)/shard_map/all_to_all | solution.py:13
  61.7 1.9 collective-permute-start
  63.6 1.5 fusion.9
  72.9 4.5 collective-permute-start.1
  77.4 5.9 constant_dynamic-slice_fusion.1
  83.3 0.0 collective-permute-done
  83.3 3.5 convolution_convert_fusion.3
  86.8 0.0 collective-permute-done.1
  86.8 2.5 convolution_convert_fusion.2
  89.3 0.0 copy-start
  89.3 6.1 fusion.2
  95.4 0.0 all-reduce.3.cloned.1.call-update
  95.4 0.0 all-reduce.5.cloned.1.call-start
  95.5 303.8 %all-reduce.3.cloned.1.call-done = f32[768,384]{1,0:T(8,128)} async-done(((f32[768,384]{1,0:T(8,128)}), f32[768,384]{1,0:T(8,128)}) %all-reduce.3.cloned.1.call-update) | async-done | bytes 1179664 | tf_op jit(solution)/shard_map/psum | solution.py:58
  399.3 0.0 copy-done
  399.3 0.8 fusion.4
  400.1 0.1 stack.15
  400.1 34.2 %all_to_all.11 = bf16[32,24,384]{2,1,0:T(8,128)(2,1)S(1)} all-to-all(bf16[32,24,384]{2,1,0:T(8,128)(2,1)S(1)} %stack.15), channel_id=1, replica_groups=mesh['kpt'=16,'aux'=32] {'aux'}, dimensions={0} | all-to-all | bytes 1179648 | tf_op jit(solution)/shard_map/all_to_all | solution.py:13
  434.4 1.9 collective-permute-start.2
  436.3 4.8 collective-permute-start.3
  441.1 8.9 %collective-permute-done.2 = bf16[768,384]{1,0:T(8,128)(2,1)S(1)} collective-permute-done((bf16[768,384]{1,0:T(8,128)(2,1)S(1)}, bf16[768,384]{1,0:T(8,128)(2,1)S(1)}, u32[]{:S(2)}, u32[]{:S(2)}) %collective-permute-start.2) | collective-permute-done | bytes 589856 | tf_op jit(solution)/shard_map/ppermute | solution.py:19
  450.0 4.1 convolution_convert_fusion.1
  454.1 0.0 collective-permute-done.3
  454.1 2.5 convolution_convert_fusion
  456.5 6.0 fusion.3
  462.6 0.0 all-reduce.5.cloned.1.call-update
  462.6 304.7 %all-reduce.5.cloned.1.call-done = f32[768,384]{1,0:T(8,128)} async-done(((f32[768,384]{1,0:T(8,128)}), f32[768,384]{1,0:T(8,128)}) %all-reduce.5.cloned.1.call-update) | async-done | bytes 1179664 | tf_op jit(solution)/shard_map/psum | solution.py:58
  767.3 1.4 subtract_bitcast_fusion
  768.7 0.6 maximum_bitcast_fusion
Async XLA Ops:
  7.2 392.1 %all-reduce.3.cloned.1.call-start = ((), (), s32[]{:S(2)}) async-start(), calls=%async_computation.2 | async-start | bytes 2359296 | tf_op jit(solution)/shard_map/psum | solution.py:58
  61.7 21.6 %collective-permute-start = (bf16[768,384]{1,0:T(8,128)(2,1)S(1)}, bf16[768,384]{1,0:T(8,128)(2,1)}, u32[]{:S(2)}, u32[]{:S(2)}) collective-permute-start(bf16[768,384]{1,0:T(8,128)(2,1)S(1)} %bitcast.49), channel_id=1, source_target_pairs={{0,32},{32,64},{64,96},{96,128},{128,160},{160,192},{192,224},{224... | collective-permute-start | bytes 1769480 | tf_op jit(solution)/shard_map/ppermute | solution.py:19
  72.9 13.9 %collective-permute-start.1 = (bf16[768,384]{1,0:T(8,128)(2,1)S(1)}, bf16[768,384]{1,0:T(8,128)(2,1)S(1)}, u32[]{:S(2)}, u32[]{:S(2)}) collective-permute-start(bf16[768,384]{1,0:T(8,128)(2,1)S(1)} %bitcast.50), channel_id=1, source_target_pairs={{0,480},{32,0},{64,32},{96,64},{128,96},{160,128},{192,160},{224,1... | collective-permute-start | bytes 1769480 | tf_op jit(solution)/shard_map/ppermute | solution.py:19
  89.3 310.0 %copy-start = (bf16[1,24,384]{2,1,0:T(8,128)(2,1)S(1)}, bf16[1,24,384]{2,1,0:T(8,128)(2,1)}, u32[]{:S(2)}) copy-start(bf16[1,24,384]{2,1,0:T(8,128)(2,1)} %param.3) | copy-start | bytes 55300
  95.4 671.9 %all-reduce.5.cloned.1.call-start = ((), (), s32[]{:S(2)}) async-start(), calls=%async_computation.3 | async-start | bytes 2359296 | tf_op jit(solution)/shard_map/psum | solution.py:58
  434.4 15.6 %collective-permute-start.2 = (bf16[768,384]{1,0:T(8,128)(2,1)S(1)}, bf16[768,384]{1,0:T(8,128)(2,1)S(1)}, u32[]{:S(2)}, u32[]{:S(2)}) collective-permute-start(bf16[768,384]{1,0:T(8,128)(2,1)S(1)} %bitcast.52), channel_id=1, source_target_pairs={{0,64},{32,96},{64,128},{96,160},{128,192},{160,224},{192,256},{22... | collective-permute-start | bytes 1769480 | tf_op jit(solution)/shard_map/ppermute | solution.py:19
  436.3 17.8 %collective-permute-start.3 = (bf16[768,384]{1,0:T(8,128)(2,1)S(1)}, bf16[768,384]{1,0:T(8,128)(2,1)S(1)}, u32[]{:S(2)}, u32[]{:S(2)}) collective-permute-start(bf16[768,384]{1,0:T(8,128)(2,1)S(1)} %bitcast.53), channel_id=1, source_target_pairs={{0,448},{32,480},{64,0},{96,32},{128,64},{160,96},{192,128},{224,1... | collective-permute-start | bytes 1769480 | tf_op jit(solution)/shard_map/ppermute | solution.py:19
Sparse Core Ops, SparseCore 0:
  95.5 303.7 all-reduce.2
  462.7 304.5 all-reduce.4
